TPU v7x, 256 devices: a whole 4x4x8 slice. The times are simulated.
256 devices in a mesh: seq: 64 (over x, z, core), head: 4 (over y).
Axes of the slice: x: 4, y: 4, z: 8, core: 2. Of those that a mesh axis runs over, the one named last changes fastest.
Arguments:
- latent: bfloat16 [64, 16, 1024], P('seq'), may hold values from -6 to 6
- stem_weight: bfloat16 [192, 3072], replicated, may hold values from -0.4375 to 0.4375
- stem_bias: float32 [3072], replicated, may hold values from -6 to 6
- mod_shift: float32 [3072], replicated, may hold values from -3 to 3
- mod_scale: float32 [3072], replicated, may hold values from -3 to 3
- qkv_weight: bfloat16 [3072, 3, 12, 128], P(None, None, 'head'), may hold values from -0.109375 to 0.109375
- q_gain: float32 [128], replicated, may hold values from 0.1 to 1.9
- k_gain: float32 [128], replicated, may hold values from 0.1 to 1.9
- tile_lists: int32 [128, 4], replicated, may hold values from 0 to 127, as said below
- out_grad: bfloat16 [16384, 12, 128], P('seq', 'head'), may hold values from -0.125 to 0.125
Outputs:
- qkv_weight_grad: float32 [3072, 3, 12, 128], P('seq', None, 'head')
- stem_weight_grad: float32 [192, 3072], P(None, 'head')
- vector_grad: float32 [3, 3072], P(None, 'head')
Inputs may be any that keep to these rules, and one draw needn't show every extreme that they name: `tile_lists`: row b holds 4 different tiles of tile b's own group of 8 tiles (b - b % 8 to b - b % 8 + 7), the first being b itself.
All inputs are finite; a program needn't handle non-finite values.
Results may differ from a plain program's by a relative error of at most 0.0078.
Values may be sent and summed in bfloat16 or wider, within the bound.
No kernel may reach another device: no remote copies, remote signals or barrier semaphores. Data moves between devices by JAX's collectives and lax.ppermute only.
A program may use at most 128 MiB of HBM per device.

v0:
```python
import jax
import jax.numpy as jnp
from jax import lax
from jax.sharding import PartitionSpec as P

TT = 2
TS = 8
KNB = 4
HG = 32
WG = 16
ln_eps = 1e-06


def swapped(value, axis, distance):
    mask = 2**distance
    pairs = [(source, source ^ mask) for source in range(lax.axis_size(axis))]
    return lax.ppermute(value, axis, pairs)


def from_behind(value, axis, steps):
    count = lax.axis_size(axis)
    first, last = (max(0, -steps), min(count, count - steps))
    return lax.ppermute(value, axis, [(source, source + steps) for source in range(first, last)])


def frames_to_tiles(blocks, row_total, col_total, tile_side):
    frames = blocks.shape[0]
    remain = blocks.shape[2:]
    shaped = blocks.reshape(
        (frames, row_total // tile_side, tile_side, col_total // tile_side, tile_side) + remain
    )
    shaped = jnp.transpose(shaped, (1, 3, 0, 2, 4) + tuple(range(5, 5 + len(remain))))
    return shaped.reshape(
        (row_total // tile_side * (col_total // tile_side), frames * tile_side * tile_side) + remain
    )


def tiles_to_frames(blocks, frames, row_total, col_total, tile_side):
    remain = blocks.shape[2:]
    shaped = blocks.reshape(
        (row_total // tile_side, col_total // tile_side, frames, tile_side, tile_side) + remain
    )
    shaped = jnp.transpose(shaped, (2, 0, 3, 1, 4) + tuple(range(5, 5 + len(remain))))
    return shaped.reshape((frames, row_total * col_total) + remain)


def qk_norm(raw_values, gain_vector):
    return (
        raw_values
        * lax.rsqrt(jnp.mean(raw_values * raw_values, -1, keepdims=True) + ln_eps)
        * gain_vector
    )


def norm_back(feature_grad, normed, inv_std, mod_scale):
    scaled = feature_grad * (1.0 + mod_scale)
    return (
        scaled
        - jnp.mean(scaled, -1, keepdims=True)
        - normed * jnp.mean(scaled * normed, -1, keepdims=True)
    ) * inv_std


def attend(queries, out_grads, key_vals, values, score_scale):
    scores = (
        jnp.einsum("brhe,bmhe->bhrm", queries, key_vals, preferred_element_type=jnp.float32)
        * score_scale
    )
    weights = jnp.exp(scores)
    probability = weights / jnp.sum(weights, axis=-1, keepdims=True)
    rounded = probability.astype(jnp.bfloat16)
    slopes = jnp.einsum("brhe,bmhe->bhrm", out_grads, values, preferred_element_type=jnp.float32)
    centre = jnp.sum(probability * slopes, axis=-1, keepdims=True)
    shaped = (probability * (slopes - centre)).astype(jnp.bfloat16)
    query_grad = (
        jnp.einsum("bhrm,bmhe->brhe", shaped, key_vals, preferred_element_type=jnp.float32)
        * score_scale
    )
    key_grad = (
        jnp.einsum("bhrm,brhe->bmhe", shaped, queries, preferred_element_type=jnp.float32)
        * score_scale
    )
    value_grad = jnp.einsum(
        "bhrm,brhe->bmhe", rounded, out_grads, preferred_element_type=jnp.float32
    )
    return (query_grad, key_grad, value_grad)


def group_share(blocks):
    seq_place = lax.axis_index("seq")
    for bit_index in range((2 * TT).bit_length() - 1):
        partner = swapped(blocks, "seq", bit_index)
        is_lower = seq_place // (1 << bit_index) % 2 == 0
        first_half = jnp.where(is_lower, blocks, partner)
        second_half = jnp.where(is_lower, partner, blocks)
        blocks = jnp.concatenate([first_half, second_half], 0)
    return blocks


def group_return(blocks):
    seq_place = lax.axis_index("seq")
    for bit_index in reversed(range((2 * TT).bit_length() - 1)):
        half_size = blocks.shape[0] // 2
        is_lower = seq_place // (1 << bit_index) % 2 == 0
        kept_part = jnp.where(is_lower, blocks[:half_size], blocks[half_size:])
        sent_part = jnp.where(is_lower, blocks[half_size:], blocks[:half_size])
        blocks = kept_part + swapped(sent_part, "seq", bit_index)
    return blocks[0]


def seq_total(stem_part, vector_part):
    return lax.psum((stem_part, vector_part), "seq")


def per_device(
    latent,
    stem_weight,
    stem_bias,
    mod_shift,
    mod_scale,
    qkv_weight,
    q_gain,
    k_gain,
    tile_lists,
    out_grad,
):
    half_rows = HG // 2
    tok_count = half_rows * WG
    frame_tokens = HG * WG
    model_width = qkv_weight.shape[0]
    heads_here = qkv_weight.shape[2]
    head_dim = qkv_weight.shape[3]
    score_scale = head_dim ** (-0.5)
    before = from_behind(latent, "seq", 2)
    after = from_behind(latent, "seq", -2)
    padded = jnp.concatenate([before, latent, after], 0)
    channels = latent.shape[1]
    patches = padded.reshape(3, channels, half_rows, 2, WG, 2)
    patches = jnp.transpose(patches, (2, 4, 0, 1, 3, 5)).reshape(tok_count, 12 * channels)
    embedded = jnp.dot(patches, stem_weight, preferred_element_type=jnp.float32) + stem_bias
    centred = embedded - jnp.mean(embedded, -1, keepdims=True)
    inv_std = lax.rsqrt(jnp.mean(centred * centred, -1, keepdims=True) + ln_eps)
    normed = centred * inv_std
    hidden = (normed * (1.0 + mod_scale) + mod_shift).astype(jnp.bfloat16)
    columns = 3 * heads_here * head_dim
    flat_weight = qkv_weight.reshape(model_width, columns)
    projected = jnp.dot(hidden, flat_weight, preferred_element_type=jnp.float32).reshape(
        tok_count, 3, heads_here, head_dim
    )
    q_normed, q_back = jax.vjp(lambda raw_values: qk_norm(raw_values, q_gain), projected[:, 0])
    k_normed, k_back = jax.vjp(lambda raw_values: qk_norm(raw_values, k_gain), projected[:, 1])
    queries = q_normed.astype(jnp.bfloat16)
    key_vals = k_normed.astype(jnp.bfloat16)
    values = projected[:, 2].astype(jnp.bfloat16)
    seq_place = lax.axis_index("seq")
    group_devs = 2 * TT
    my_group = seq_place // group_devs
    my_half = seq_place % 2
    tiles_group = HG // TS * (WG // TS)
    half_tiles = tiles_group // 2
    local_lists = (
        lax.dynamic_slice_in_dim(tile_lists, my_group * tiles_group, tiles_group, 0)
        - my_group * tiles_group
    )
    shared = group_share(jnp.stack([key_vals, values], 1)[None])
    shared = shared.reshape((TT, frame_tokens) + shared.shape[2:])
    tiles = frames_to_tiles(shared, HG, WG, TS)
    tile_len = tiles.shape[1]
    my_lists = lax.dynamic_slice_in_dim(local_lists, my_half * half_tiles, half_tiles, 0)
    near_tiles = jnp.take(tiles, my_lists.reshape(-1), axis=0)
    near_tiles = near_tiles.reshape(half_tiles, KNB * tile_len, 2, heads_here, head_dim)
    own_queries = frames_to_tiles(queries[None], half_rows, WG, TS)
    own_grads = frames_to_tiles(out_grad[None], half_rows, WG, TS)
    query_part, key_part, value_part = attend(
        own_queries, own_grads, near_tiles[:, :, 0], near_tiles[:, :, 1], score_scale
    )
    query_grad = tiles_to_frames(query_part, 1, half_rows, WG, TS)[0]
    pair_part = jnp.stack([key_part, value_part], 2).reshape(
        half_tiles * KNB, tile_len, 2, heads_here, head_dim
    )
    pair_tiles = (
        jnp.zeros((tiles_group, tile_len, 2, heads_here, head_dim), jnp.float32)
        .at[my_lists.reshape(-1)]
        .add(pair_part)
    )
    framed = tiles_to_frames(pair_tiles, TT, HG, WG, TS)
    returned = group_return(framed.reshape((group_devs, tok_count) + framed.shape[2:]))
    key_grad = returned[:, 0]
    value_grad = returned[:, 1]
    raw_q = q_back(query_grad)[0]
    raw_k = k_back(key_grad)[0]
    mixed_grad = (
        jnp.stack([raw_q, raw_k, value_grad], 1).astype(jnp.bfloat16).reshape(tok_count, columns)
    )
    weight_grad = lax.psum_scatter(
        lax.dot_general(
            hidden, mixed_grad, (((0,), (0,)), ((), ())), preferred_element_type=jnp.float32
        ),
        "seq",
        scatter_dimension=0,
        tiled=True,
    )
    weight_grad = weight_grad.reshape(-1, 3, heads_here, head_dim)
    feature_grad = lax.dot_general(
        mixed_grad, flat_weight, (((1,), (1,)), ((), ())), preferred_element_type=jnp.float32
    )
    patch_rows = patches.astype(jnp.float32)
    feature_grad = lax.psum(feature_grad, "head")
    embed_grad = norm_back(feature_grad, normed, inv_std, mod_scale)
    share_cols = model_width // lax.axis_size("head")
    offset = lax.axis_index("head") * share_cols
    grad_slice = lax.dynamic_slice_in_dim(feature_grad, offset, share_cols, 1)
    normed_slice = lax.dynamic_slice_in_dim(normed, offset, share_cols, 1)
    embed_slice = lax.dynamic_slice_in_dim(embed_grad, offset, share_cols, 1)
    stem_part = lax.dot_general(
        patch_rows, embed_slice, (((0,), (0,)), ((), ())), precision=lax.Precision.HIGHEST
    )
    vector_part = jnp.stack(
        [jnp.sum(grad_slice, 0), jnp.sum(grad_slice * normed_slice, 0), jnp.sum(embed_slice, 0)]
    )
    stem_grad, vector_grad = seq_total(stem_part, vector_part)
    return (weight_grad, stem_grad, vector_grad)


def solution(mesh):
    return jax.shard_map(
        per_device,
        mesh=mesh,
        in_specs=(
            P("seq", None, None),
            P(),
            P(),
            P(),
            P(),
            P(None, None, "head", None),
            P(),
            P(),
            P(),
            P("seq", "head", None),
        ),
        out_specs=(P("seq", None, "head", None), P(None, "head"), P(None, "head")),
        check_vma=False,
    )
```

profile of v0, /device:TPU:8, one launch (start us, length us, event | category | flops | bytes accessed | tf_op | source)
XLA Modules:
  0.0 514.7 jit_solution(13901229938263370222)
XLA Ops:
  8.1 4.0 collective-permute-start
  12.0 1.3 collective-permute-start.1
  13.3 0.7 broadcast_add_fusion
  14.0 10.3 %copy.44 = bf16[3072,3,3,128]{0,3,2,1:T(8,128)(2,1)} copy(bf16[3072,3,3,128]{3,0,2,1:T(8,128)(2,1)} %param.15) | data formatting | bytes 14155776 | tf_op args[5]
  24.7 1.7 copy.42
  26.4 0.7 reshape.189
  27.1 0.7 fusion.29
  28.3 1.1 copy-done.2
  29.4 0.5 subtract_multiply_fusion
  30.4 0.9 slice-done.3
  31.3 2.3 fusion
  34.0 0.7 copy-done.8
  35.6 1.1 collective-permute-done.2
  36.9 2.9 collective-permute-start.3
  40.2 17.6 %collective-permute-done.3 = bf16[2,256,2,3,128]{4,1,3,2,0:T(8,128)(2,1)} collective-permute-done((bf16[2,256,2,3,128]{4,1,3,2,0:T(8,128)(2,1)S(1)}, bf16[2,256,2,3,128]{4,1,3,2,0:T(8,128)(2,1)}, u32[]{:S(2)}, u32[]{:S(2)}) %collective-permute-start.3) | collective-permute-done | bytes 786464 | tf_op jit(solution)/shard_map/ppermute | solution.py:17
  57.7 1.2 broadcast_select_fusion.1
  59.7 2.6 gather_fusion
  62.3 2.3 copy.48
  64.6 0.5 copy_select_fusion
  65.1 0.7 fusion.2
  65.8 1.0 copy-done.6
  66.8 0.7 multiply_exponential_fusion
  67.5 3.3 convolution_bitcast_fusion.1
  70.8 2.1 fusion.4
  73.0 1.9 copy.54
  75.2 0.9 copy-done.11
  76.0 0.6 multiply_bitcast_fusion
  76.7 2.3 copy.53
  79.0 3.3 pad_maximum_fusion
  82.3 3.1 copy.55
  85.7 9.3 %scatter_fusion = f32[8,128,2,3,128]{4,1,3,2,0:T(8,128)S(1)} fusion(f32[8,128,2,3,128]{4,1,3,2,0:T(8,128)S(1)} %broadcast_in_dim.47, s32[16]{0:T(128)S(1)} %fusion.24, f32[16,128,2,3,128]{4,1,3,2,0:T(8,128)} %copy.55), kind=kCustom, calls=%fused_computation.1 | custom fusion | flops 1572864 | bytes 18874432 | tf_op jit(solution)/shard_map/scatter-add | solution.py:184
  95.9 1.8 collective-permute-start.4
  97.7 34.2 %collective-permute-done.4 = f32[2,256,2,3,128]{4,1,3,2,0:T(8,128)S(1)} collective-permute-done((f32[2,256,2,3,128]{4,1,3,2,0:T(8,128)S(1)}, f32[2,256,2,3,128]{4,1,3,2,0:T(8,128)S(1)}, u32[]{:S(2)}, u32[]{:S(2)}) %collective-permute-start.4) | collective-permute-done | bytes 1572896 | tf_op jit(solution)/shard_map/ppermute | solution.py:17
  132.3 1.8 copy-done.7
  135.6 0.6 copy-done.13
  136.3 4.0 convolution_bitcast_fusion
  140.6 2.1 maximum_convert_fusion
  142.7 2.1 copy.59
  144.8 8.4 %fusion.14 = f32[3072,1152]{1,0:T(8,128)} fusion(bf16[256,1152]{0,1:T(8,128)(2,1)} %bitcast.148, f32[256,3072]{1,0:T(8,128)S(1)} %copy-done.5, f32[3072]{0:T(1024)S(1)} %copy-done.17, f32[3072]{0:T(1024)S(1)} %broadcast_add_fusion), kind=kOutput, calls=%fused_computation.48 | convolution fusion | flops 1814298624 | bytes 17915904 | tf_op jit(solution)/shard_map/dot_general | solution.py:196
  153.3 70.6 %all-reduce.3.cloned.1.call-done = f32[256,3072]{1,0:T(8,128)} async-done(((f32[256,3072]{1,0:T(8,128)}), f32[256,3072]{1,0:T(8,128)}) %all-reduce.3.cloned.1.call-update) | async-done | bytes 3145744 | tf_op jit(solution)/shard_map/psum | solution.py:208
  223.9 2.9 fusion.26
  226.8 1.7 dynamic-slice_reduce_fusion
  228.5 1.3 fusion.30
  229.9 252.3 %psum.23 = f32[3,768]{1,0:T(4,128)} all-reduce(f32[3,768]{1,0:T(4,128)S(1)} %pad_maximum_fusion.4), channel_id=1, replica_groups=mesh['seq'=64,'head'=4] {'seq'}, use_global_device_ids=true, to_apply=%region_17.18 | all-reduce | flops 2304 | bytes 18432 | tf_op jit(solution)/shard_map/psum | solution.py:112
  482.2 1.0 reshape.197
  483.3 0.7 copy.60
  484.0 21.3 %all-reduce.5.cloned.1.call-done = f32[192,768]{1,0:T(8,128)} async-done(((f32[192,768]{1,0:T(8,128)}), f32[192,768]{1,0:T(8,128)}) %all-reduce.5.cloned.1.call-update) | async-done | bytes 589840 | tf_op jit(solution)/shard_map/psum | solution.py:112
  505.3 1.9 copy.73
  (109 shorter events, 7.6 us)
Async XLA Ops:
  8.0 19.1 %copy-start = (bf16[192,3072]{1,0:T(8,128)(2,1)S(1)}, bf16[192,3072]{1,0:T(8,128)(2,1)}, u32[]{:S(2)}) copy-start(bf16[192,3072]{1,0:T(8,128)(2,1)} %param.11) | copy-start | bytes 3538948
  8.0 215.9 %all-reduce.3.cloned.1.call-start = ((), (), s32[]{:S(2)}) async-start(), calls=%async_computation.2 | async-start | bytes 6291456 | tf_op jit(solution)/shard_map/psum | solution.py:208
  8.1 16.3 %collective-permute-start = (bf16[1,16,1024]{2,1,0:T(8,128)(2,1)}, bf16[1,16,1024]{2,1,0:T(8,128)(2,1)S(1)}, u32[]{:S(2)}, u32[]{:S(2)}) collective-permute-start(bf16[1,16,1024]{2,1,0:T(8,128)(2,1)} %param.10), channel_id=1, source_target_pairs={{0,8},{4,12},{8,16},{12,20},{16,24},{20,28},{24,32},{28,36},{32,40... | collective-permute-start | bytes 98312 | tf_op jit(solution)/shard_map/ppermute | solution.py:23
  12.0 12.3 %collective-permute-start.1 = (bf16[1,16,1024]{2,1,0:T(8,128)(2,1)}, bf16[1,16,1024]{2,1,0:T(8,128)(2,1)S(1)}, u32[]{:S(2)}, u32[]{:S(2)}) collective-permute-start(bf16[1,16,1024]{2,1,0:T(8,128)(2,1)} %param.10), channel_id=1, source_target_pairs={{8,0},{12,4},{16,8},{20,12},{24,16},{28,20},{32,24},{36,28},{40,32... | collective-permute-start | bytes 98312 | tf_op jit(solution)/shard_map/ppermute | solution.py:23
  14.0 10.3 %copy-start.18 = (bf16[1,16,1024]{2,1,0:T(8,128)(2,1)S(1)}, bf16[1,16,1024]{2,1,0:T(8,128)(2,1)}, u32[]{:S(2)}) copy-start(bf16[1,16,1024]{2,1,0:T(8,128)(2,1)} %param.10) | copy-start | bytes 98308
  24.3 2.8 copy-start.19
  27.1 3.3 slice-start.2
  27.8 1.6 copy-start.2
  27.8 3.5 slice-start.3
  29.4 1.9 copy-start.17
  31.3 2.3 copy-start.4
  31.3 3.4 copy-start.20
  33.6 1.1 copy-start.8
  33.6 1.4 copy-start.22
  33.6 1.9 copy-start.16
  33.9 6.0 %copy-start.21 = (f32[128]{0:T(128)S(1)}, f32[128]{0:T(128)}, u32[]{:S(2)}) copy-start(f32[128]{0:T(128)} %param.16) | copy-start | bytes 1540
  34.9 1.8 collective-permute-start.2
  35.6 29.5 %copy-start.15 = (bf16[2,2,1,8,8,3,128]{6,4,3,5,1,0,2:T(8,128)(2,1)}, bf16[2,2,1,8,8,3,128]{6,4,3,5,1,0,2:T(8,128)(2,1)S(1)}, u32[]{:S(2)}) copy-start(bf16[2,2,1,8,8,3,128]{6,4,3,5,1,0,2:T(8,128)(2,1)S(1)} %copy.51) | copy-start | bytes 589828
  36.9 20.9 %collective-permute-start.3 = (bf16[2,256,2,3,128]{4,1,3,2,0:T(8,128)(2,1)S(1)}, bf16[2,256,2,3,128]{4,1,3,2,0:T(8,128)(2,1)}, u32[]{:S(2)}, u32[]{:S(2)}) collective-permute-start(bf16[2,256,2,3,128]{4,1,3,2,0:T(8,128)(2,1)S(1)} %pad_maximum_fusion.2), channel_id=1, source_target_pairs={{0,8},{4,12},{8,0},{12,4},{16,24},{20,28},{24,16},{28,20},{32,40},... | collective-permute-start | bytes 2359304 | tf_op jit(solution)/shard_map/ppermute | solution.py:17
  65.1 1.7 copy-start.6
  70.8 2.1 copy-start.10
  75.2 0.9 copy-start.11
  95.7 36.6 %copy-start.12 = (bf16[4,3,64,512]{3,2,1,0:T(8,128)(2,1)S(1)}, bf16[4,3,64,512]{3,2,1,0:T(8,128)(2,1)}, u32[]{:S(2)}) copy-start(bf16[4,3,64,512]{3,2,1,0:T(8,128)(2,1)} %copy-done.11) | copy-start | bytes 2359300
  95.9 36.0 %collective-permute-start.4 = (f32[2,256,2,3,128]{4,1,3,2,0:T(8,128)S(1)}, f32[2,256,2,3,128]{4,1,3,2,0:T(8,128)S(1)}, u32[]{:S(2)}, u32[]{:S(2)}) collective-permute-start(f32[2,256,2,3,128]{4,1,3,2,0:T(8,128)S(1)} %copy.57), channel_id=1, source_target_pairs={{0,8},{4,12},{8,0},{12,4},{16,24},{20,28},{24,16},{28,20},{32,40},... | collective-permute-start | bytes 4718600 | tf_op jit(solution)/shard_map/ppermute | solution.py:17
  131.9 2.2 copy-start.7
  131.9 4.5 slice-start
  132.2 2.6 copy-start.9
  132.2 4.1 slice-start.1
  132.2 2.4 collective-permute-start.5
  135.6 0.7 copy-start.13
  135.6 0.7 copy-start.14
  140.3 4.5 copy-start.5
  140.3 341.9 %reduce-scatter.2.cloned.1.call-start = ((), (), s32[]{:S(2)}) async-start(), calls=%async_computation.1 | async-start | bytes 14376960 | tf_op jit(solution)/shard_map/reduce_scatter | solution.py:195
  153.2 70.7 %copy-start.3 = (f32[256,3072]{1,0:T(8,128)S(1)}, f32[256,3072]{1,0:T(8,128)}, u32[]{:S(2)}) copy-start(f32[256,3072]{1,0:T(8,128)} %copy-done.2) | copy-start | bytes 9437188
  153.2 352.1 %all-reduce.5.cloned.1.call-start = ((), (), s32[]{:S(2)}) async-start(), calls=%async_computation.3 | async-start | bytes 1179648 | tf_op jit(solution)/shard_map/psum | solution.py:112
  226.8 280.5 %copy-start.1 = (bf16[192,3072]{1,0:T(8,128)(2,1)S(1)}, bf16[192,3072]{1,0:T(8,128)(2,1)}, u32[]{:S(2)}) copy-start(bf16[192,3072]{1,0:T(8,128)(2,1)} %param.11) | copy-start | bytes 3538948
Sparse Core Ops, SparseCore 0:
  140.5 83.3 all-reduce.2
Sparse Core Ops, SparseCore 1:
  153.3 168.1 reduce-scatter.1
  325.3 179.9 all-reduce.4
where the time goes:
time: 516 us; the launch traced here: 515 us
  blocking collectives  252 us (49%)
  waiting for transfers between devices  145 us (28%)
  local copies, waits for them, and re-layouts  40.5 us (8%)
  other arithmetic  28 us (5%)
  matrix products  22.3 us (4%)
  between operations  16.1 us (3%)
  starting transfers between devices  10.5 us (2%)
    psum x1, blocking collectives, seq_total(): return lax.psum((stem_part, vector_part), 'seq')  252 us
    psum x1, waiting for transfers between devices, per_device(): feature_grad = lax.psum(feature_grad, 'head')  70.6 us
    ppermute x4, waiting for transfers between devices, swapped(): return lax.ppermute(value, axis, pairs)  52.9 us
    psum x1, waiting for transfers between devices, seq_total(): return lax.psum((stem_part, vector_part), 'seq')  21.3 us
    unnamed x59, local copies, waits for them, and re-layouts  20.7 us
  transfers between devices with their start and end apart: 9, of which 5 were waited for; matrix products, arithmetic and copies ran while one was open for 6% of the time, Pallas kernels for 0%

commit v1 on v0

--- a/solution.py
+++ b/solution.py
@@ -9,6 +9,14 @@
 HG = 32
 WG = 16
 ln_eps = 1e-06
+
+
+def added_up(x, name):
+    size, total = (lax.axis_size(name), x)
+    for stride in [1 << k for k in range(size.bit_length() - 1)]:
+        swap = [(i, i ^ stride) for i in range(size)]
+        total = total + lax.ppermute(total, name, swap)
+    return total
 
 
 def swapped(value, axis, distance):
@@ -205,7 +213,7 @@
         mixed_grad, flat_weight, (((1,), (1,)), ((), ())), preferred_element_type=jnp.float32
     )
     patch_rows = patches.astype(jnp.float32)
-    feature_grad = lax.psum(feature_grad, "head")
+    feature_grad = added_up(feature_grad, "head")
     embed_grad = norm_back(feature_grad, normed, inv_std, mod_scale)
     share_cols = model_width // lax.axis_size("head")
     offset = lax.axis_index("head") * share_cols

time: 516 us -> 567 us (1.099)
  waiting for transfers between devices: 145 us -> 192 us
    ppermute x0 -> x2, waiting for transfers between devices: none -> 139 us  [added_up(): total = total + lax.ppermute(total, name, swap)]
    psum x1 -> x0, waiting for transfers between devices: 70.6 us -> none  [per_device(): feature_grad = lax.psum(feature_grad, 'head')]
    psum x1, waiting for transfers between devices: 21.3 us -> 0.01 us  [seq_total(): return lax.psum((stem_part, vector_part), 'seq')]
  transfers between devices with their start and end apart: 9 -> 10, of which waited for: 5 -> 6; matrix products, arithmetic and copies ran while one was open for 6% -> 5% of each run, Pallas kernels for 0% -> 0%
where the time goes in v1:
time: 567 us; the launch traced here: 566 us
  blocking collectives  252 us (44%)
  waiting for transfers between devices  192 us (34%)
  local copies, waits for them, and re-layouts  41.1 us (7%)
  other arithmetic  29.9 us (5%)
  matrix products  23.6 us (4%)
  between operations  14.7 us (3%)
  starting transfers between devices  13.3 us (2%)
    psum x1, blocking collectives, seq_total(): return lax.psum((stem_part, vector_part), 'seq')  252 us
    ppermute x2, waiting for transfers between devices, added_up(): total = total + lax.ppermute(total, name, swap)  139 us
    ppermute x4, waiting for transfers between devices, swapped(): return lax.ppermute(value, axis, pairs)  53.2 us
    unnamed x59, local copies, waits for them, and re-layouts  21.2 us
  transfers between devices with their start and end apart: 10, of which 6 were waited for; matrix products, arithmetic and copies ran while one was open for 5% of the time, Pallas kernels for 0%

profile of v1, /device:TPU:8, one launch (start us, length us, event | category | flops | bytes accessed | tf_op | source)
XLA Modules:
  0.0 566.2 jit_solution(9737625891737487773)
XLA Ops:
  7.2 4.0 collective-permute-start
  11.2 1.3 collective-permute-start.1
  12.5 0.7 broadcast_add_fusion
  13.2 10.3 %copy.44 = bf16[3072,3,3,128]{0,3,2,1:T(8,128)(2,1)} copy(bf16[3072,3,3,128]{3,0,2,1:T(8,128)(2,1)} %param.15) | data formatting | bytes 14155776 | tf_op args[5]
  23.9 1.7 copy.42
  25.6 0.7 reshape.189
  26.3 0.7 fusion.29
  27.5 1.1 copy-done.2
  29.6 0.9 slice-done.1
  30.5 2.3 fusion
  33.1 0.7 copy-done.8
  34.8 1.1 collective-permute-done.2
  36.0 2.9 collective-permute-start.3
  39.3 17.6 %collective-permute-done.3 = bf16[2,256,2,3,128]{4,1,3,2,0:T(8,128)(2,1)} collective-permute-done((bf16[2,256,2,3,128]{4,1,3,2,0:T(8,128)(2,1)S(1)}, bf16[2,256,2,3,128]{4,1,3,2,0:T(8,128)(2,1)}, u32[]{:S(2)}, u32[]{:S(2)}) %collective-permute-start.3) | collective-permute-done | bytes 786464 | tf_op jit(solution)/shard_map/ppermute | solution.py:25
  56.9 1.2 broadcast_select_fusion.1
  58.9 2.6 gather_fusion
  61.5 2.3 copy.48
  64.3 0.7 fusion.2
  65.0 1.0 copy-done.6
  66.0 0.7 multiply_exponential_fusion
  66.7 3.3 convolution_bitcast_fusion.1
  70.0 2.1 fusion.4
  72.1 1.9 copy.54
  74.3 0.9 copy-done.11
  75.8 2.3 copy.53
  78.2 3.3 pad_maximum_fusion
  81.4 3.1 copy.55
  84.9 9.3 %scatter_fusion = f32[8,128,2,3,128]{4,1,3,2,0:T(8,128)S(1)} fusion(f32[8,128,2,3,128]{4,1,3,2,0:T(8,128)S(1)} %broadcast_in_dim.47, s32[16]{0:T(128)S(1)} %fusion.24, f32[16,128,2,3,128]{4,1,3,2,0:T(8,128)} %copy.55), kind=kCustom, calls=%fused_computation.1 | custom fusion | flops 1572864 | bytes 18874432 | tf_op jit(solution)/shard_map/scatter-add | solution.py:192
  95.0 1.8 collective-permute-start.4
  96.9 34.2 %collective-permute-done.4 = f32[2,256,2,3,128]{4,1,3,2,0:T(8,128)S(1)} collective-permute-done((f32[2,256,2,3,128]{4,1,3,2,0:T(8,128)S(1)}, f32[2,256,2,3,128]{4,1,3,2,0:T(8,128)S(1)}, u32[]{:S(2)}, u32[]{:S(2)}) %collective-permute-start.4) | collective-permute-done | bytes 1572896 | tf_op jit(solution)/shard_map/ppermute | solution.py:25
  131.7 1.2 copy-done.7
  135.0 0.7 copy-done.13
  135.7 0.9 maximum_convert_fusion
  136.6 2.1 copy.59
  138.7 8.4 %fusion.14 = f32[3072,1152]{1,0:T(8,128)} fusion(bf16[256,1152]{0,1:T(8,128)(2,1)} %bitcast.146, f32[256,3072]{1,0:T(8,128)S(1)} %copy-done.5, f32[3072]{0:T(1024)S(1)} %copy-done.19, f32[3072]{0:T(1024)S(1)} %broadcast_add_fusion), kind=kOutput, calls=%fused_computation.48 | convolution fusion | flops 1814298624 | bytes 17915904 | tf_op jit(solution)/shard_map/dot_general | solution.py:204
  147.2 0.8 copy-done.14
  148.1 5.3 convolution_bitcast_fusion
  153.9 69.7 %collective-permute-done.6 = f32[256,3072]{1,0:T(8,128)S(1)} collective-permute-done((f32[256,3072]{1,0:T(8,128)S(1)}, f32[256,3072]{1,0:T(8,128)S(1)}, u32[]{:S(2)}, u32[]{:S(2)}) %collective-permute-start.6) | collective-permute-done | bytes 3145760 | tf_op jit(solution)/shard_map/ppermute | solution.py:18
  223.6 2.2 add.131
  225.8 2.3 collective-permute-start.7
  228.2 68.8 %collective-permute-done.7 = f32[256,3072]{1,0:T(8,128)} collective-permute-done((f32[256,3072]{1,0:T(8,128)}, f32[256,3072]{1,0:T(8,128)}, u32[]{:S(2)}, u32[]{:S(2)}) %collective-permute-start.7) | collective-permute-done | bytes 3145760 | tf_op jit(solution)/shard_map/ppermute | solution.py:18
  297.0 3.9 fusion.26
  300.9 1.5 dynamic-slice_reduce_fusion
  302.5 1.3 fusion.30
  303.8 251.8 %psum.15 = f32[3,768]{1,0:T(4,128)} all-reduce(f32[3,768]{1,0:T(4,128)S(1)} %pad_maximum_fusion.4), channel_id=1, replica_groups=mesh['seq'=64,'head'=4] {'seq'}, use_global_device_ids=true, to_apply=%region_16.17 | all-reduce | flops 2304 | bytes 18432 | tf_op jit(solution)/shard_map/psum | solution.py:120
  555.7 1.0 reshape.197
  556.7 0.7 copy.60
  557.4 1.9 copy.72
  (110 shorter events, 10.4 us)
Async XLA Ops:
  7.2 19.1 %copy-start = (bf16[192,3072]{1,0:T(8,128)(2,1)S(1)}, bf16[192,3072]{1,0:T(8,128)(2,1)}, u32[]{:S(2)}) copy-start(bf16[192,3072]{1,0:T(8,128)(2,1)} %param.11) | copy-start | bytes 3538948
  7.2 548.5 %reduce-scatter.2.cloned.1.call-start = ((), (), s32[]{:S(2)}) async-start(), calls=%async_computation.1 | async-start | bytes 14376960 | tf_op jit(solution)/shard_map/reduce_scatter | solution.py:203
  7.2 16.3 %collective-permute-start = (bf16[1,16,1024]{2,1,0:T(8,128)(2,1)}, bf16[1,16,1024]{2,1,0:T(8,128)(2,1)S(1)}, u32[]{:S(2)}, u32[]{:S(2)}) collective-permute-start(bf16[1,16,1024]{2,1,0:T(8,128)(2,1)} %param.10), channel_id=1, source_target_pairs={{0,8},{4,12},{8,16},{12,20},{16,24},{20,28},{24,32},{28,36},{32,40... | collective-permute-start | bytes 98312 | tf_op jit(solution)/shard_map/ppermute | solution.py:31
  11.2 12.3 %collective-permute-start.1 = (bf16[1,16,1024]{2,1,0:T(8,128)(2,1)}, bf16[1,16,1024]{2,1,0:T(8,128)(2,1)S(1)}, u32[]{:S(2)}, u32[]{:S(2)}) collective-permute-start(bf16[1,16,1024]{2,1,0:T(8,128)(2,1)} %param.10), channel_id=1, source_target_pairs={{8,0},{12,4},{16,8},{20,12},{24,16},{28,20},{32,24},{36,28},{40,32... | collective-permute-start | bytes 98312 | tf_op jit(solution)/shard_map/ppermute | solution.py:31
  13.2 10.3 %copy-start.20 = (bf16[1,16,1024]{2,1,0:T(8,128)(2,1)S(1)}, bf16[1,16,1024]{2,1,0:T(8,128)(2,1)}, u32[]{:S(2)}) copy-start(bf16[1,16,1024]{2,1,0:T(8,128)(2,1)} %param.10) | copy-start | bytes 98308
  23.5 2.8 copy-start.21
  26.3 3.3 slice-start
  27.0 1.6 copy-start.2
  27.0 3.5 slice-start.1
  28.6 1.9 copy-start.19
  30.5 2.3 copy-start.4
  30.5 3.4 copy-start.22
  32.8 1.1 copy-start.8
  32.8 1.4 copy-start.24
  32.8 1.9 copy-start.18
  33.1 6.0 %copy-start.23 = (f32[128]{0:T(128)S(1)}, f32[128]{0:T(128)}, u32[]{:S(2)}) copy-start(f32[128]{0:T(128)} %param.16) | copy-start | bytes 1540
  34.1 1.8 collective-permute-start.2
  34.8 29.5 %copy-start.17 = (bf16[2,2,1,8,8,3,128]{6,4,3,5,1,0,2:T(8,128)(2,1)}, bf16[2,2,1,8,8,3,128]{6,4,3,5,1,0,2:T(8,128)(2,1)S(1)}, u32[]{:S(2)}) copy-start(bf16[2,2,1,8,8,3,128]{6,4,3,5,1,0,2:T(8,128)(2,1)S(1)} %copy.51) | copy-start | bytes 589828
  36.0 20.9 %collective-permute-start.3 = (bf16[2,256,2,3,128]{4,1,3,2,0:T(8,128)(2,1)S(1)}, bf16[2,256,2,3,128]{4,1,3,2,0:T(8,128)(2,1)}, u32[]{:S(2)}, u32[]{:S(2)}) collective-permute-start(bf16[2,256,2,3,128]{4,1,3,2,0:T(8,128)(2,1)S(1)} %pad_maximum_fusion.2), channel_id=1, source_target_pairs={{0,8},{4,12},{8,0},{12,4},{16,24},{20,28},{24,16},{28,20},{32,40},... | collective-permute-start | bytes 2359304 | tf_op jit(solution)/shard_map/ppermute | solution.py:25
  64.3 1.7 copy-start.6
  70.0 2.1 copy-start.10
  74.3 0.9 copy-start.11
  95.0 36.0 %collective-permute-start.4 = (f32[2,256,2,3,128]{4,1,3,2,0:T(8,128)S(1)}, f32[2,256,2,3,128]{4,1,3,2,0:T(8,128)S(1)}, u32[]{:S(2)}, u32[]{:S(2)}) collective-permute-start(f32[2,256,2,3,128]{4,1,3,2,0:T(8,128)S(1)} %copy.57), channel_id=1, source_target_pairs={{0,8},{4,12},{8,0},{12,4},{16,24},{20,28},{24,16},{28,20},{32,40},... | collective-permute-start | bytes 4718600 | tf_op jit(solution)/shard_map/ppermute | solution.py:25
  131.0 1.9 copy-start.7
  131.0 2.1 copy-start.12
  131.4 2.8 copy-start.9
  131.4 2.6 collective-permute-start.5
  134.2 4.5 copy-start.5
  135.0 0.7 copy-start.13
  135.0 0.7 copy-start.15
  147.1 0.9 copy-start.14
  147.1 1.0 copy-start.16
  147.1 410.2 %all-reduce.2.cloned.1.call-start = ((), (), s32[]{:S(2)}) async-start(), calls=%async_computation.2 | async-start | bytes 1179648 | tf_op jit(solution)/shard_map/psum | solution.py:120
  153.4 143.6 %copy-start.3 = (f32[256,3072]{1,0:T(8,128)S(1)}, f32[256,3072]{1,0:T(8,128)}, u32[]{:S(2)}) copy-start(f32[256,3072]{1,0:T(8,128)} %copy-done.2) | copy-start | bytes 9437188
  153.4 70.2 %collective-permute-start.6 = (f32[256,3072]{1,0:T(8,128)S(1)}, f32[256,3072]{1,0:T(8,128)S(1)}, u32[]{:S(2)}, u32[]{:S(2)}) collective-permute-start(f32[256,3072]{1,0:T(8,128)S(1)} %convolution_bitcast_fusion), channel_id=1, source_target_pairs={{0,1},{1,0},{2,3},{3,2},{4,5},{5,4},{6,7},{7,6},{8,9},{9,8},{10,11... | collective-permute-start | bytes 9437192 | tf_op jit(solution)/shard_map/ppermute | solution.py:18
  225.8 71.1 %collective-permute-start.7 = (f32[256,3072]{1,0:T(8,128)}, f32[256,3072]{1,0:T(8,128)}, u32[]{:S(2)}, u32[]{:S(2)}) collective-permute-start(f32[256,3072]{1,0:T(8,128)} %add.131), channel_id=1, source_target_pairs={{0,2},{1,3},{2,0},{3,1},{4,6},{5,7},{6,4},{7,5},{8,10},{9,11},{10,... | collective-permute-start | bytes 9437192 | tf_op jit(solution)/shard_map/ppermute | solution.py:18
  300.9 258.4 %copy-start.1 = (bf16[192,3072]{1,0:T(8,128)(2,1)S(1)}, bf16[192,3072]{1,0:T(8,128)(2,1)}, u32[]{:S(2)}) copy-start(bf16[192,3072]{1,0:T(8,128)(2,1)} %param.11) | copy-start | bytes 3538948
Sparse Core Ops, SparseCore 0:
  147.3 168.0 reduce-scatter.1
  319.4 180.8 all-reduce.1
